TPU v7x, 32 devices: a whole 2x2x4 slice. The times are simulated.
32 devices in a mesh: gx: 4 (over x, core), gy: 8 (over z, y).
Axes of the slice: x: 2, y: 2, z: 4, core: 2. Of those that a mesh axis runs over, the one named last changes fastest.
Arguments:
- probes: float32 [32, 64, 64, 256], P(None, 'gx', 'gy'), may hold values from -108 to 108, as said below
- diffusion: float32 [64, 64, 256], P('gx', 'gy'), may hold values from 0.03 to 0.16
- velocity: float32 [3, 64, 64, 256], P(None, 'gx', 'gy'), may hold values from -0.2 to 0.2
Outputs:
- basis: float32 [32, 64, 64, 256], P(None, 'gx', 'gy')
- factor: float32 [32, 32], replicated
Inputs may be any that keep to these rules, and one draw needn't show every extreme that they name: `probes`: each entry is finite and real-valued.
All inputs are finite; a program needn't handle non-finite values.
Results may differ from a plain program's by a relative error of at most 0.00011.
Values sent between devices are 32-bit elements; how exact they have to be, the bound alone decides.
No kernel may reach another device: no remote copies, remote signals or barrier semaphores. Data moves between devices by JAX's collectives and lax.ppermute only.
A program may use at most 64 MiB of HBM per device.

v0:
```python
import jax
import jax.numpy as jnp
from jax import lax
from jax.sharding import PartitionSpec as P

STEPS = 2


def with_halo(cells, sides, width):
    for axis, dim in sides:
        count = lax.axis_size(axis)
        ends = count - 1
        head = lax.slice_in_dim(cells, 0, width, axis=dim)
        tail = lax.slice_in_dim(cells, cells.shape[dim] - width, cells.shape[dim], axis=dim)
        cells = jnp.concatenate(
            [
                lax.ppermute(tail, axis, [(i, (i + 1) % count) for i in range(ends)]),
                cells,
                lax.ppermute(head, axis, [((i + 1) % count, i) for i in range(ends)]),
            ],
            axis=dim,
        )
    return cells


def stencil_step(padded, diffusion, velocity):
    center = padded[:, 1:-1, 1:-1, :]
    deeper = jnp.pad(center, ((0, 0), (0, 0), (0, 0), (1, 1)))
    result = (1.0 - 6.0 * diffusion) * center
    result = (
        result
        + (diffusion - 0.5 * velocity[0]) * padded[:, 2:, 1:-1, :]
        + (diffusion + 0.5 * velocity[0]) * padded[:, :-2, 1:-1, :]
    )
    result = (
        result
        + (diffusion - 0.5 * velocity[1]) * padded[:, 1:-1, 2:, :]
        + (diffusion + 0.5 * velocity[1]) * padded[:, 1:-1, :-2, :]
    )
    result = (
        result
        + (diffusion - 0.5 * velocity[2]) * deeper[:, :, :, 2:]
        + (diffusion + 0.5 * velocity[2]) * deeper[:, :, :, :-2]
    )
    return result


def on_device(probes, diffusion, velocity):
    field = probes
    for sweep_index in range(STEPS):
        padded = with_halo(field, (("gx", 1), ("gy", 2)), 1)
        field = stencil_step(padded, diffusion, velocity)
    probe_count = field.shape[0]
    flat = field.reshape(probe_count, -1)
    total_cells = flat.shape[1] * lax.axis_size("gx") * lax.axis_size("gy")
    local_gram = jnp.dot(
        flat, flat.T, precision=lax.Precision.HIGHEST, preferred_element_type=jnp.float32
    )
    gram = lax.psum(local_gram, ("gx", "gy")) * (1.0 / total_cells)
    lower = jnp.linalg.cholesky(gram)
    basis = jax.scipy.linalg.solve_triangular(lower, flat, lower=True)
    return (basis.reshape(field.shape), lower.T)


def solution(mesh):
    return jax.shard_map(
        on_device,
        mesh=mesh,
        in_specs=(P(None, "gx", "gy", None), P("gx", "gy", None), P(None, "gx", "gy", None)),
        out_specs=(P(None, "gx", "gy", None), P()),
        check_vma=False,
    )
```

profile of v0, /device:TPU:0, one launch (start us, length us, event | category | flops | bytes accessed | tf_op | source)
XLA Modules:
  0.0 177.1 jit_solution(3824144828677573553)
XLA Ops:
  0.6 4.8 %copy.33 = f32[32,16,8,256]{3,0,2,1:T(8,128)S(1)} copy(f32[32,16,8,256]{3,2,1,0:T(8,128)} %param.3) | data formatting | bytes 8388608 | tf_op args[0]
  5.5 2.4 %collective-permute-start.1 = (f32[32,1,8,256]{3,0,2,1:T(8,128)S(1)}, f32[32,1,8,256]{3,0,2,1:T(8,128)S(1)}, u32[]{:S(2)}, u32[]{:S(2)}) collective-permute-start(f32[32,1,8,256]{3,0,2,1:T(8,128)S(1)} %get-tuple-element.17), channel_id=1, source_target_pairs={{0,8},{8,16},{16,24},{1,9},{9,17},{17,25},{2,10},{10,18},{18,26},{... | collective-permute-start | bytes 786440 | tf_op jit(solution)/shard_map/ppermute | solution.py:17
  7.8 1.3 collective-permute-start
  9.2 2.7 %constant_dynamic-update-slice_fusion.1 = f32[32,18,8,256]{3,0,2,1:T(8,128)S(1)} fusion(f32[32,18,8,256]{3,0,2,1:T(8,128)S(1)} %constant_dynamic-update-slice_fusion.2, f32[32,16,8,256]{3,2,1,0:T(8,128)S(1)} %copy-done.2), kind=kLoop, calls=%fused_computation.66 | loop fusion | bytes 8388608
  11.9 1.4 collective-permute-done
  13.4 0.1 fusion.29
  13.5 1.3 collective-permute-start.2
  14.8 4.6 %collective-permute-start.3 = (f32[32,18,1,256]{3,0,2,1:T(8,128)S(1)}, f32[32,18,1,256]{3,0,2,1:T(8,128)S(1)}, u32[]{:S(2)}, u32[]{:S(2)}) collective-permute-start(f32[32,18,1,256]{3,0,2,1:T(8,128)S(1)} %get-tuple-element.13), channel_id=1, source_target_pairs={{0,1},{1,2},{2,3},{3,4},{4,5},{5,6},{6,7},{8,9},{9,10},{10,11},{11... | collective-permute-start | bytes 1769480 | tf_op jit(solution)/shard_map/ppermute | solution.py:17
  19.4 0.1 bitcast_subtract_fusion.2
  19.5 8.2 %collective-permute-done.2 = f32[32,18,1,256]{3,0,2,1:T(8,128)S(1)} collective-permute-done((f32[32,18,1,256]{3,0,2,1:T(8,128)S(1)}, f32[32,18,1,256]{3,0,2,1:T(8,128)S(1)}, u32[]{:S(2)}, u32[]{:S(2)}) %collective-permute-start.2) | collective-permute-done | bytes 589856 | tf_op jit(solution)/shard_map/ppermute | solution.py:19
  27.7 16.3 %collective-permute-done.3 = f32[32,18,1,256]{3,0,2,1:T(8,128)S(1)} collective-permute-done((f32[32,18,1,256]{3,0,2,1:T(8,128)S(1)}, f32[32,18,1,256]{3,0,2,1:T(8,128)S(1)}, u32[]{:S(2)}, u32[]{:S(2)}) %collective-permute-start.3) | collective-permute-done | bytes 589856 | tf_op jit(solution)/shard_map/ppermute | solution.py:17
  44.1 9.5 %fusion.2 = f32[32,16,8,256]{3,0,2,1:T(8,128)S(1)} fusion(f32[32,16,8,256]{3,0,2,1:T(8,128)S(1)} %copy.33, f32[32,18,8,256]{3,0,2,1:T(8,128)} %copy-done.3, f32[32,18,1,256]{3,0,2,1:T(8,128)S(1)} %collective-permute-done.3, f32[32,18,1,256]{3,0,2,1:T(8,128)S(1)} %collective-permute-done.2, f32[32,1,8,256]{3,0,2,1:T(8,128)S(1)} %collective-permute-done.1, ...), kind=kLoop, calls=%fused_computation.6 | loop fusion | flops 17825792 | bytes 15728640 | tf_op jit(solution)/shard_map/add | solution.py:41
  53.6 2.2 %collective-permute-start.5 = (f32[32,1,8,256]{3,0,2,1:T(8,128)S(1)}, f32[32,1,8,256]{3,0,2,1:T(8,128)S(1)}, u32[]{:S(2)}, u32[]{:S(2)}) collective-permute-start(f32[32,1,8,256]{3,0,2,1:T(8,128)S(1)} %get-tuple-element.14), channel_id=1, source_target_pairs={{0,8},{8,16},{16,24},{1,9},{9,17},{17,25},{2,10},{10,18},{18,26},{... | collective-permute-start | bytes 786440 | tf_op jit(solution)/shard_map/ppermute | solution.py:17
  55.8 1.3 collective-permute-start.4
  57.1 2.7 %collective-permute-done.4 = f32[32,1,8,256]{3,0,2,1:T(8,128)S(1)} collective-permute-done((f32[32,1,8,256]{3,0,2,1:T(8,128)S(1)}, f32[32,1,8,256]{3,0,2,1:T(8,128)S(1)}, u32[]{:S(2)}, u32[]{:S(2)}) %collective-permute-start.4) | collective-permute-done | bytes 262176 | tf_op jit(solution)/shard_map/ppermute | solution.py:19
  59.9 0.1 pad_maximum_fusion.14
  60.0 1.3 collective-permute-start.6
  61.3 5.2 %collective-permute-start.7 = (f32[32,18,1,256]{3,0,2,1:T(8,128)S(1)}, f32[32,18,1,256]{3,0,2,1:T(8,128)S(1)}, u32[]{:S(2)}, u32[]{:S(2)}) collective-permute-start(f32[32,18,1,256]{3,0,2,1:T(8,128)S(1)} %get-tuple-element.11), channel_id=1, source_target_pairs={{0,1},{1,2},{2,3},{3,4},{4,5},{5,6},{6,7},{8,9},{9,10},{10,11},{11... | collective-permute-start | bytes 1769480 | tf_op jit(solution)/shard_map/ppermute | solution.py:17
  66.5 7.9 %collective-permute-done.6 = f32[32,18,1,256]{3,0,2,1:T(8,128)S(1)} collective-permute-done((f32[32,18,1,256]{3,0,2,1:T(8,128)S(1)}, f32[32,18,1,256]{3,0,2,1:T(8,128)S(1)}, u32[]{:S(2)}, u32[]{:S(2)}) %collective-permute-start.6) | collective-permute-done | bytes 589856 | tf_op jit(solution)/shard_map/ppermute | solution.py:19
  74.4 17.1 %collective-permute-done.7 = f32[32,18,1,256]{3,0,2,1:T(8,128)S(1)} collective-permute-done((f32[32,18,1,256]{3,0,2,1:T(8,128)S(1)}, f32[32,18,1,256]{3,0,2,1:T(8,128)S(1)}, u32[]{:S(2)}, u32[]{:S(2)}) %collective-permute-start.7) | collective-permute-done | bytes 589856 | tf_op jit(solution)/shard_map/ppermute | solution.py:17
  91.5 17.3 %fusion.6 = f32[32,16,8,256]{3,0,2,1:T(8,128)S(1)} fusion(f32[32,16,8,256]{3,0,2,1:T(8,128)} %copy-done.1, f32[32,18,1,256]{3,0,2,1:T(8,128)S(1)} %collective-permute-done.7, f32[32,1,8,256]{3,0,2,1:T(8,128)S(1)} %collective-permute-done.4, f32[32,1,8,256]{3,0,2,1:T(8,128)S(1)} %collective-permute-done.5, f32[32,18,1,256]{3,0,2,1:T(8,128)S(1)} %collective-permute-done.6, ...), kind=kLoop, calls=%fused_computation.10 | loop fusion | flops 22020096 | bytes 11010048 | tf_op jit(solution)/shard_map/add | solution.py:41
  108.9 2.0 %copy-done = f32[32,16,8,256]{3,0,2,1:T(8,128)} copy-done((f32[32,16,8,256]{3,0,2,1:T(8,128)}, f32[32,16,8,256]{3,0,2,1:T(8,128)S(1)}, u32[]{:S(2)}) %copy-start) | copy-done | bytes 4194328
  110.9 3.4 %convolution_bitcast_fusion = f32[32,32]{0,1:T(8,128)S(1)} fusion(f32[32,16,8,256]{3,0,2,1:T(8,128)S(1)} %fusion.6), kind=kOutput, calls=%fused_computation.42 | convolution fusion | flops 402653184 | bytes 4198400 | tf_op jit(solution)/shard_map/dot_general | solution.py:56
  114.3 40.3 %psum.7 = f32[32,32]{0,1:T(8,128)S(1)} all-reduce(f32[32,32]{0,1:T(8,128)S(1)} %convolution_bitcast_fusion), channel_id=1, replica_groups=mesh['gx'=4,'gy'=8] {'gx','gy'}, use_global_device_ids=true, to_apply=%region_0.1 | all-reduce | flops 1024 | bytes 8192 | tf_op jit(solution)/shard_map/psum | solution.py:59
  154.7 2.9 %cholesky.16 = f32[32,32]{1,0:T(8,128)S(1)} custom-call(f32[32,32]{1,0:T(8,128)S(1)} %fusion.27), custom_call_target="Cholesky" | custom-call | tf_op jit(solution)/shard_map/jit(cholesky)/cholesky | solution.py:60
  157.7 0.6 compare_reduce_fusion
  158.3 0.7 fusion.28
  159.0 0.7 copy.46
  159.6 2.4 %custom-call.7 = f32[1,32,32]{1,2,0:T(8,128)S(1)} custom-call(f32[1,32,32]{2,1,0:T(8,128)S(1)} %get-tuple-element.26), custom_call_target="InvertDiagBlocksLowerTriangular" | custom-call | tf_op jit(solution)/shard_map/jit(_solve_triangular)/triangular_solve | solution.py:61
  162.1 4.6 %copy.52 = f32[4,8,128,256]{3,2,1,0:T(8,128)S(1)} copy(f32[4,8,128,256]{3,1,0,2:T(8,128)} %bitcast.37) | data formatting | bytes 8388608
  166.7 5.9 %fusion.24 = f32[32,16,8,256]{3,0,2,1:T(8,128)S(1)} fusion(f32[16,8,256,32]{2,1,0,3:T(8,128)S(1)} %bitcast.38, f32[1,32,32]{1,2,0:T(8,128)S(1)} %custom-call.7), kind=kOutput, calls=%fused_computation.40 | convolution fusion | flops 402653184 | bytes 8392704 | tf_op jit(solution)/shard_map/jit(_solve_triangular)/triangular_solve | solution.py:61
  172.7 4.4 %copy.45 = f32[32,16,8,256]{3,2,1,0:T(8,128)} copy(f32[32,16,8,256]{3,0,2,1:T(8,128)S(1)} %fusion.24) | data formatting | bytes 8388608
  (21 shorter events, 0.3 us)
Async XLA Ops:
  0.6 8.5 %copy-start.2 = (f32[32,16,8,256]{3,2,1,0:T(8,128)S(1)}, f32[32,16,8,256]{3,2,1,0:T(8,128)}, u32[]{:S(2)}) copy-start(f32[32,16,8,256]{3,2,1,0:T(8,128)} %param.3) | copy-start | bytes 12582916
  5.5 3.7 %collective-permute-start.1 = (f32[32,1,8,256]{3,0,2,1:T(8,128)S(1)}, f32[32,1,8,256]{3,0,2,1:T(8,128)S(1)}, u32[]{:S(2)}, u32[]{:S(2)}) collective-permute-start(f32[32,1,8,256]{3,0,2,1:T(8,128)S(1)} %get-tuple-element.17), channel_id=1, source_target_pairs={{0,8},{8,16},{16,24},{1,9},{9,17},{17,25},{2,10},{10,18},{18,26},{... | collective-permute-start | bytes 786440 | tf_op jit(solution)/shard_map/ppermute | solution.py:17
  7.8 5.5 %collective-permute-start = (f32[32,1,8,256]{3,0,2,1:T(8,128)S(1)}, f32[32,1,8,256]{3,0,2,1:T(8,128)S(1)}, u32[]{:S(2)}, u32[]{:S(2)}) collective-permute-start(f32[32,1,8,256]{3,0,2,1:T(8,128)S(1)} %get-tuple-element.16), channel_id=1, source_target_pairs={{8,0},{16,8},{24,16},{9,1},{17,9},{25,17},{10,2},{18,10},{26,18},{... | collective-permute-start | bytes 786440 | tf_op jit(solution)/shard_map/ppermute | solution.py:19
  9.2 10.2 %copy-start.4 = (f32[3,16,8,256]{3,2,1,0:T(8,128)S(1)}, f32[3,16,8,256]{3,2,1,0:T(8,128)}, u32[]{:S(2)}) copy-start(f32[3,16,8,256]{3,2,1,0:T(8,128)} %param.5) | copy-start | bytes 1179652
  9.2 10.2 %copy-start.5 = (f32[16,8,256]{2,1,0:T(8,128)S(1)}, f32[16,8,256]{2,1,0:T(8,128)}, u32[]{:S(2)}) copy-start(f32[16,8,256]{2,1,0:T(8,128)} %param.4) | copy-start | bytes 393220
  13.4 30.7 %copy-start.3 = (f32[32,18,8,256]{3,0,2,1:T(8,128)}, f32[32,18,8,256]{3,0,2,1:T(8,128)S(1)}, u32[]{:S(2)}) copy-start(f32[32,18,8,256]{3,0,2,1:T(8,128)S(1)} %constant_dynamic-update-slice_fusion) | copy-start | bytes 14155780
  13.5 14.2 %collective-permute-start.2 = (f32[32,18,1,256]{3,0,2,1:T(8,128)S(1)}, f32[32,18,1,256]{3,0,2,1:T(8,128)S(1)}, u32[]{:S(2)}, u32[]{:S(2)}) collective-permute-start(f32[32,18,1,256]{3,0,2,1:T(8,128)S(1)} %get-tuple-element.12), channel_id=1, source_target_pairs={{1,0},{2,1},{3,2},{4,3},{5,4},{6,5},{7,6},{9,8},{10,9},{11,10},{12... | collective-permute-start | bytes 1769480 | tf_op jit(solution)/shard_map/ppermute | solution.py:19
  14.8 29.3 %collective-permute-start.3 = (f32[32,18,1,256]{3,0,2,1:T(8,128)S(1)}, f32[32,18,1,256]{3,0,2,1:T(8,128)S(1)}, u32[]{:S(2)}, u32[]{:S(2)}) collective-permute-start(f32[32,18,1,256]{3,0,2,1:T(8,128)S(1)} %get-tuple-element.13), channel_id=1, source_target_pairs={{0,1},{1,2},{2,3},{3,4},{4,5},{5,6},{6,7},{8,9},{9,10},{10,11},{11... | collective-permute-start | bytes 1769480 | tf_op jit(solution)/shard_map/ppermute | solution.py:17
  53.5 20.9 %copy-start.1 = (f32[32,16,8,256]{3,0,2,1:T(8,128)}, f32[32,16,8,256]{3,0,2,1:T(8,128)S(1)}, u32[]{:S(2)}) copy-start(f32[32,16,8,256]{3,0,2,1:T(8,128)S(1)} %fusion.2) | copy-start | bytes 12582916
  53.6 3.5 %collective-permute-start.5 = (f32[32,1,8,256]{3,0,2,1:T(8,128)S(1)}, f32[32,1,8,256]{3,0,2,1:T(8,128)S(1)}, u32[]{:S(2)}, u32[]{:S(2)}) collective-permute-start(f32[32,1,8,256]{3,0,2,1:T(8,128)S(1)} %get-tuple-element.14), channel_id=1, source_target_pairs={{0,8},{8,16},{16,24},{1,9},{9,17},{17,25},{2,10},{10,18},{18,26},{... | collective-permute-start | bytes 786440 | tf_op jit(solution)/shard_map/ppermute | solution.py:17
  55.8 4.1 %collective-permute-start.4 = (f32[32,1,8,256]{3,0,2,1:T(8,128)S(1)}, f32[32,1,8,256]{3,0,2,1:T(8,128)S(1)}, u32[]{:S(2)}, u32[]{:S(2)}) collective-permute-start(f32[32,1,8,256]{3,0,2,1:T(8,128)S(1)} %get-tuple-element.15), channel_id=1, source_target_pairs={{8,0},{16,8},{24,16},{9,1},{17,9},{25,17},{10,2},{18,10},{26,18},{... | collective-permute-start | bytes 786440 | tf_op jit(solution)/shard_map/ppermute | solution.py:19
  60.0 14.4 %collective-permute-start.6 = (f32[32,18,1,256]{3,0,2,1:T(8,128)S(1)}, f32[32,18,1,256]{3,0,2,1:T(8,128)S(1)}, u32[]{:S(2)}, u32[]{:S(2)}) collective-permute-start(f32[32,18,1,256]{3,0,2,1:T(8,128)S(1)} %get-tuple-element.10), channel_id=1, source_target_pairs={{1,0},{2,1},{3,2},{4,3},{5,4},{6,5},{7,6},{9,8},{10,9},{11,10},{12... | collective-permute-start | bytes 1769480 | tf_op jit(solution)/shard_map/ppermute | solution.py:19
  61.3 30.2 %collective-permute-start.7 = (f32[32,18,1,256]{3,0,2,1:T(8,128)S(1)}, f32[32,18,1,256]{3,0,2,1:T(8,128)S(1)}, u32[]{:S(2)}, u32[]{:S(2)}) collective-permute-start(f32[32,18,1,256]{3,0,2,1:T(8,128)S(1)} %get-tuple-element.11), channel_id=1, source_target_pairs={{0,1},{1,2},{2,3},{3,4},{4,5},{5,6},{6,7},{8,9},{9,10},{10,11},{11... | collective-permute-start | bytes 1769480 | tf_op jit(solution)/shard_map/ppermute | solution.py:17
  108.9 2.0 %copy-start = (f32[32,16,8,256]{3,0,2,1:T(8,128)}, f32[32,16,8,256]{3,0,2,1:T(8,128)S(1)}, u32[]{:S(2)}) copy-start(f32[32,16,8,256]{3,0,2,1:T(8,128)S(1)} %fusion.6) | copy-start | bytes 12582916
where the time goes:
time: 178 us; the launch traced here: 177 us
  waiting for transfers between devices  53.8 us (30%)
  blocking collectives  40.3 us (23%)
  other arithmetic  33.7 us (19%)
  local copies, waits for them, and re-layouts  19.6 us (11%)
  starting transfers between devices  19.6 us (11%)
  matrix products  9.3 us (5%)
    psum x1, blocking collectives, on_device(): gram = lax.psum(local_gram, ('gx', 'gy')) * (1.0 / total_cells)  40.3 us
    ppermute x4, waiting for transfers between devices, with_halo(): lax.ppermute(tail, axis, [(i, (i + 1) % count) for i in range(ends)])  33.4 us
    add x2, other arithmetic, stencil_step(): result + (diffusion - 0.5 * velocity[2]) * deeper[:, :, :, 2:]  26.8 us
    ppermute x4, waiting for transfers between devices, with_halo(): lax.ppermute(head, axis, [((i + 1) % count, i) for i in range(ends)])  20.3 us
    unnamed x18, local copies, waits for them, and re-layouts  19.3 us
    ppermute x4, starting transfers between devices, with_halo(): lax.ppermute(tail, axis, [(i, (i + 1) % count) for i in range(ends)])  14.4 us
    another operation x1, matrix products, on_device(): basis = jax.scipy.linalg.solve_triangular(lower, flat, lower=True)  5.92 us
    ppermute x4, starting transfers between devices, with_halo(): lax.ppermute(head, axis, [((i + 1) % count, i) for i in range(ends)])  5.17 us
  transfers between devices with their start and end apart: 8, of which 6 were waited for; matrix products, arithmetic and copies ran while one was open for 2% of the time, Pallas kernels for 0%

commit v1 on v0

--- a/solution.py
+++ b/solution.py
@@ -1,9 +1,19 @@
+import functools
 import jax
 import jax.numpy as jnp
 from jax import lax
 from jax.sharding import PartitionSpec as P
 
 STEPS = 2
+
+
+def point_seats_all_over_axis(chunk, row_axis, named_axis):
+    for src_i in (row_axis, named_axis):
+        chunk = lax.psum(chunk, src_i)
+    return chunk
+
+
+treat_cycles = functools.partial(point_seats_all_over_axis, row_axis="gy", named_axis="gx")
 
 
 def with_halo(cells, sides, width):
@@ -56,7 +66,7 @@
     local_gram = jnp.dot(
         flat, flat.T, precision=lax.Precision.HIGHEST, preferred_element_type=jnp.float32
     )
-    gram = lax.psum(local_gram, ("gx", "gy")) * (1.0 / total_cells)
+    gram = treat_cycles(local_gram) * (1.0 / total_cells)
     lower = jnp.linalg.cholesky(gram)
     basis = jax.scipy.linalg.solve_triangular(lower, flat, lower=True)
     return (basis.reshape(field.shape), lower.T)

time: 178 us -> 183 us (1.028)
  blocking collectives: 40.3 us -> 45.9 us
    psum x1 -> x2, blocking collectives: 40.3 us -> 45.9 us  [point_seats_all_over_axis(): chunk = lax.psum(chunk, src_i)]
where the time goes in v1:
time: 183 us
  waiting for transfers between devices  53.8 us (29%)
  blocking collectives  45.9 us (25%)
  other arithmetic  33.7 us (18%)
  local copies, waits for them, and re-layouts  19.6 us (11%)
  starting transfers between devices  19.6 us (11%)
  matrix products  9.3 us (5%)
    psum x2, blocking collectives, point_seats_all_over_axis(): chunk = lax.psum(chunk, src_i)  45.9 us
    ppermute x4, waiting for transfers between devices, with_halo(): lax.ppermute(tail, axis, [(i, (i + 1) % count) for i in range(ends)])  33.4 us
    add x2, other arithmetic, stencil_step(): result + (diffusion - 0.5 * velocity[2]) * deeper[:, :, :, 2:]  26.8 us
    ppermute x4, waiting for transfers between devices, with_halo(): lax.ppermute(head, axis, [((i + 1) % count, i) for i in range(ends)])  20.3 us
    unnamed x18, local copies, waits for them, and re-layouts  19.3 us
    ppermute x4, starting transfers between devices, with_halo(): lax.ppermute(tail, axis, [(i, (i + 1) % count) for i in range(ends)])  14.4 us
    another operation x1, matrix products, on_device(): basis = jax.scipy.linalg.solve_triangular(lower, flat, lower=True)  5.92 us
    ppermute x4, starting transfers between devices, with_halo(): lax.ppermute(head, axis, [((i + 1) % count, i) for i in range(ends)])  5.17 us
  transfers between devices with their start and end apart: 8, of which 6 were waited for; matrix products, arithmetic and copies ran while one was open for 2% of the time, Pallas kernels for 0%

profile of v1, /device:TPU:0, one launch (start us, length us, event | category | flops | bytes accessed | tf_op | source)
XLA Modules:
  0.0 182.6 jit_solution(4213184962818356073)
XLA Ops:
  0.6 4.8 %copy.33 = f32[32,16,8,256]{3,0,2,1:T(8,128)S(1)} copy(f32[32,16,8,256]{3,2,1,0:T(8,128)} %param.3) | data formatting | bytes 8388608 | tf_op args[0]
  5.5 2.4 %collective-permute-start.1 = (f32[32,1,8,256]{3,0,2,1:T(8,128)S(1)}, f32[32,1,8,256]{3,0,2,1:T(8,128)S(1)}, u32[]{:S(2)}, u32[]{:S(2)}) collective-permute-start(f32[32,1,8,256]{3,0,2,1:T(8,128)S(1)} %get-tuple-element.17), channel_id=1, source_target_pairs={{0,8},{8,16},{16,24},{1,9},{9,17},{17,25},{2,10},{10,18},{18,26},{... | collective-permute-start | bytes 786440 | tf_op jit(solution)/shard_map/ppermute | solution.py:27
  7.8 1.3 collective-permute-start
  9.2 2.7 %constant_dynamic-update-slice_fusion.1 = f32[32,18,8,256]{3,0,2,1:T(8,128)S(1)} fusion(f32[32,18,8,256]{3,0,2,1:T(8,128)S(1)} %constant_dynamic-update-slice_fusion.2, f32[32,16,8,256]{3,2,1,0:T(8,128)S(1)} %copy-done.2), kind=kLoop, calls=%fused_computation.66 | loop fusion | bytes 8388608
  11.9 1.4 collective-permute-done
  13.4 0.1 fusion.29
  13.5 1.3 collective-permute-start.2
  14.8 4.6 %collective-permute-start.3 = (f32[32,18,1,256]{3,0,2,1:T(8,128)S(1)}, f32[32,18,1,256]{3,0,2,1:T(8,128)S(1)}, u32[]{:S(2)}, u32[]{:S(2)}) collective-permute-start(f32[32,18,1,256]{3,0,2,1:T(8,128)S(1)} %get-tuple-element.13), channel_id=1, source_target_pairs={{0,1},{1,2},{2,3},{3,4},{4,5},{5,6},{6,7},{8,9},{9,10},{10,11},{11... | collective-permute-start | bytes 1769480 | tf_op jit(solution)/shard_map/ppermute | solution.py:27
  19.5 8.2 %collective-permute-done.2 = f32[32,18,1,256]{3,0,2,1:T(8,128)S(1)} collective-permute-done((f32[32,18,1,256]{3,0,2,1:T(8,128)S(1)}, f32[32,18,1,256]{3,0,2,1:T(8,128)S(1)}, u32[]{:S(2)}, u32[]{:S(2)}) %collective-permute-start.2) | collective-permute-done | bytes 589856 | tf_op jit(solution)/shard_map/ppermute | solution.py:29
  27.7 16.3 %collective-permute-done.3 = f32[32,18,1,256]{3,0,2,1:T(8,128)S(1)} collective-permute-done((f32[32,18,1,256]{3,0,2,1:T(8,128)S(1)}, f32[32,18,1,256]{3,0,2,1:T(8,128)S(1)}, u32[]{:S(2)}, u32[]{:S(2)}) %collective-permute-start.3) | collective-permute-done | bytes 589856 | tf_op jit(solution)/shard_map/ppermute | solution.py:27
  44.1 9.5 %fusion.2 = f32[32,16,8,256]{3,0,2,1:T(8,128)S(1)} fusion(f32[32,16,8,256]{3,0,2,1:T(8,128)S(1)} %copy.33, f32[32,18,8,256]{3,0,2,1:T(8,128)} %copy-done.3, f32[32,18,1,256]{3,0,2,1:T(8,128)S(1)} %collective-permute-done.3, f32[32,18,1,256]{3,0,2,1:T(8,128)S(1)} %collective-permute-done.2, f32[32,1,8,256]{3,0,2,1:T(8,128)S(1)} %collective-permute-done.1, ...), kind=kLoop, calls=%fused_computation.6 | loop fusion | flops 17825792 | bytes 15728640 | tf_op jit(solution)/shard_map/add | solution.py:51
  53.6 2.2 %collective-permute-start.5 = (f32[32,1,8,256]{3,0,2,1:T(8,128)S(1)}, f32[32,1,8,256]{3,0,2,1:T(8,128)S(1)}, u32[]{:S(2)}, u32[]{:S(2)}) collective-permute-start(f32[32,1,8,256]{3,0,2,1:T(8,128)S(1)} %get-tuple-element.14), channel_id=1, source_target_pairs={{0,8},{8,16},{16,24},{1,9},{9,17},{17,25},{2,10},{10,18},{18,26},{... | collective-permute-start | bytes 786440 | tf_op jit(solution)/shard_map/ppermute | solution.py:27
  55.8 1.3 collective-permute-start.4
  57.1 2.7 %collective-permute-done.4 = f32[32,1,8,256]{3,0,2,1:T(8,128)S(1)} collective-permute-done((f32[32,1,8,256]{3,0,2,1:T(8,128)S(1)}, f32[32,1,8,256]{3,0,2,1:T(8,128)S(1)}, u32[]{:S(2)}, u32[]{:S(2)}) %collective-permute-start.4) | collective-permute-done | bytes 262176 | tf_op jit(solution)/shard_map/ppermute | solution.py:29
  59.9 0.1 pad_maximum_fusion.14
  60.0 1.3 collective-permute-start.6
  61.3 5.2 %collective-permute-start.7 = (f32[32,18,1,256]{3,0,2,1:T(8,128)S(1)}, f32[32,18,1,256]{3,0,2,1:T(8,128)S(1)}, u32[]{:S(2)}, u32[]{:S(2)}) collective-permute-start(f32[32,18,1,256]{3,0,2,1:T(8,128)S(1)} %get-tuple-element.11), channel_id=1, source_target_pairs={{0,1},{1,2},{2,3},{3,4},{4,5},{5,6},{6,7},{8,9},{9,10},{10,11},{11... | collective-permute-start | bytes 1769480 | tf_op jit(solution)/shard_map/ppermute | solution.py:27
  66.5 7.9 %collective-permute-done.6 = f32[32,18,1,256]{3,0,2,1:T(8,128)S(1)} collective-permute-done((f32[32,18,1,256]{3,0,2,1:T(8,128)S(1)}, f32[32,18,1,256]{3,0,2,1:T(8,128)S(1)}, u32[]{:S(2)}, u32[]{:S(2)}) %collective-permute-start.6) | collective-permute-done | bytes 589856 | tf_op jit(solution)/shard_map/ppermute | solution.py:29
  74.4 17.1 %collective-permute-done.7 = f32[32,18,1,256]{3,0,2,1:T(8,128)S(1)} collective-permute-done((f32[32,18,1,256]{3,0,2,1:T(8,128)S(1)}, f32[32,18,1,256]{3,0,2,1:T(8,128)S(1)}, u32[]{:S(2)}, u32[]{:S(2)}) %collective-permute-start.7) | collective-permute-done | bytes 589856 | tf_op jit(solution)/shard_map/ppermute | solution.py:27
  91.5 17.3 %fusion.6 = f32[32,16,8,256]{3,0,2,1:T(8,128)S(1)} fusion(f32[32,16,8,256]{3,0,2,1:T(8,128)} %copy-done.1, f32[32,18,1,256]{3,0,2,1:T(8,128)S(1)} %collective-permute-done.7, f32[32,1,8,256]{3,0,2,1:T(8,128)S(1)} %collective-permute-done.4, f32[32,1,8,256]{3,0,2,1:T(8,128)S(1)} %collective-permute-done.5, f32[32,18,1,256]{3,0,2,1:T(8,128)S(1)} %collective-permute-done.6, ...), kind=kLoop, calls=%fused_computation.10 | loop fusion | flops 22020096 | bytes 11010048 | tf_op jit(solution)/shard_map/add | solution.py:51
  108.9 2.0 %copy-done = f32[32,16,8,256]{3,0,2,1:T(8,128)} copy-done((f32[32,16,8,256]{3,0,2,1:T(8,128)}, f32[32,16,8,256]{3,0,2,1:T(8,128)S(1)}, u32[]{:S(2)}) %copy-start) | copy-done | bytes 4194328
  110.9 3.4 %convolution_bitcast_fusion = f32[32,32]{0,1:T(8,128)S(1)} fusion(f32[32,16,8,256]{3,0,2,1:T(8,128)S(1)} %fusion.6), kind=kOutput, calls=%fused_computation.42 | convolution fusion | flops 402653184 | bytes 4198400 | tf_op jit(solution)/shard_map/dot_general | solution.py:66
  114.3 35.6 %psum.14 = f32[32,32]{0,1:T(8,128)S(1)} all-reduce(f32[32,32]{0,1:T(8,128)S(1)} %convolution_bitcast_fusion), channel_id=1, replica_groups=mesh['gx'=4,'gy'=8] {'gy'}, use_global_device_ids=true, to_apply=%region_0.1 | all-reduce | flops 1024 | bytes 8192 | tf_op jit(solution)/shard_map/psum | solution.py:12
  149.8 10.3 %psum.15 = f32[32,32]{0,1:T(8,128)S(1)} all-reduce(f32[32,32]{0,1:T(8,128)S(1)} %psum.14), channel_id=1, replica_groups=mesh['gx'=4,'gy'=8] {'gx'}, use_global_device_ids=true, to_apply=%region_1.2 | all-reduce | flops 1024 | bytes 8192 | tf_op jit(solution)/shard_map/psum | solution.py:12
  160.3 2.9 %cholesky.16 = f32[32,32]{1,0:T(8,128)S(1)} custom-call(f32[32,32]{1,0:T(8,128)S(1)} %fusion.27), custom_call_target="Cholesky" | custom-call | tf_op jit(solution)/shard_map/jit(cholesky)/cholesky | solution.py:70
  163.2 0.6 compare_reduce_fusion
  163.9 0.7 fusion.28
  164.5 0.7 copy.46
  165.2 2.4 %custom-call.7 = f32[1,32,32]{1,2,0:T(8,128)S(1)} custom-call(f32[1,32,32]{2,1,0:T(8,128)S(1)} %get-tuple-element.26), custom_call_target="InvertDiagBlocksLowerTriangular" | custom-call | tf_op jit(solution)/shard_map/jit(_solve_triangular)/triangular_solve | solution.py:71
  167.6 4.6 %copy.52 = f32[4,8,128,256]{3,2,1,0:T(8,128)S(1)} copy(f32[4,8,128,256]{3,1,0,2:T(8,128)} %bitcast.37) | data formatting | bytes 8388608
  172.3 5.9 %fusion.24 = f32[32,16,8,256]{3,0,2,1:T(8,128)S(1)} fusion(f32[16,8,256,32]{2,1,0,3:T(8,128)S(1)} %bitcast.38, f32[1,32,32]{1,2,0:T(8,128)S(1)} %custom-call.7), kind=kOutput, calls=%fused_computation.40 | convolution fusion | flops 402653184 | bytes 8392704 | tf_op jit(solution)/shard_map/jit(_solve_triangular)/triangular_solve | solution.py:71
  178.2 4.4 %copy.45 = f32[32,16,8,256]{3,2,1,0:T(8,128)} copy(f32[32,16,8,256]{3,0,2,1:T(8,128)S(1)} %fusion.24) | data formatting | bytes 8388608
  (22 shorter events, 0.4 us)
Async XLA Ops:
  0.6 8.5 %copy-start.2 = (f32[32,16,8,256]{3,2,1,0:T(8,128)S(1)}, f32[32,16,8,256]{3,2,1,0:T(8,128)}, u32[]{:S(2)}) copy-start(f32[32,16,8,256]{3,2,1,0:T(8,128)} %param.3) | copy-start | bytes 12582916
  5.5 3.7 %collective-permute-start.1 = (f32[32,1,8,256]{3,0,2,1:T(8,128)S(1)}, f32[32,1,8,256]{3,0,2,1:T(8,128)S(1)}, u32[]{:S(2)}, u32[]{:S(2)}) collective-permute-start(f32[32,1,8,256]{3,0,2,1:T(8,128)S(1)} %get-tuple-element.17), channel_id=1, source_target_pairs={{0,8},{8,16},{16,24},{1,9},{9,17},{17,25},{2,10},{10,18},{18,26},{... | collective-permute-start | bytes 786440 | tf_op jit(solution)/shard_map/ppermute | solution.py:27
  7.8 5.5 %collective-permute-start = (f32[32,1,8,256]{3,0,2,1:T(8,128)S(1)}, f32[32,1,8,256]{3,0,2,1:T(8,128)S(1)}, u32[]{:S(2)}, u32[]{:S(2)}) collective-permute-start(f32[32,1,8,256]{3,0,2,1:T(8,128)S(1)} %get-tuple-element.16), channel_id=1, source_target_pairs={{8,0},{16,8},{24,16},{9,1},{17,9},{25,17},{10,2},{18,10},{26,18},{... | collective-permute-start | bytes 786440 | tf_op jit(solution)/shard_map/ppermute | solution.py:29
  9.2 10.2 %copy-start.4 = (f32[3,16,8,256]{3,2,1,0:T(8,128)S(1)}, f32[3,16,8,256]{3,2,1,0:T(8,128)}, u32[]{:S(2)}) copy-start(f32[3,16,8,256]{3,2,1,0:T(8,128)} %param.5) | copy-start | bytes 1179652
  9.2 10.2 %copy-start.5 = (f32[16,8,256]{2,1,0:T(8,128)S(1)}, f32[16,8,256]{2,1,0:T(8,128)}, u32[]{:S(2)}) copy-start(f32[16,8,256]{2,1,0:T(8,128)} %param.4) | copy-start | bytes 393220
  13.4 30.7 %copy-start.3 = (f32[32,18,8,256]{3,0,2,1:T(8,128)}, f32[32,18,8,256]{3,0,2,1:T(8,128)S(1)}, u32[]{:S(2)}) copy-start(f32[32,18,8,256]{3,0,2,1:T(8,128)S(1)} %constant_dynamic-update-slice_fusion) | copy-start | bytes 14155780
  13.5 14.2 %collective-permute-start.2 = (f32[32,18,1,256]{3,0,2,1:T(8,128)S(1)}, f32[32,18,1,256]{3,0,2,1:T(8,128)S(1)}, u32[]{:S(2)}, u32[]{:S(2)}) collective-permute-start(f32[32,18,1,256]{3,0,2,1:T(8,128)S(1)} %get-tuple-element.12), channel_id=1, source_target_pairs={{1,0},{2,1},{3,2},{4,3},{5,4},{6,5},{7,6},{9,8},{10,9},{11,10},{12... | collective-permute-start | bytes 1769480 | tf_op jit(solution)/shard_map/ppermute | solution.py:29
  14.8 29.3 %collective-permute-start.3 = (f32[32,18,1,256]{3,0,2,1:T(8,128)S(1)}, f32[32,18,1,256]{3,0,2,1:T(8,128)S(1)}, u32[]{:S(2)}, u32[]{:S(2)}) collective-permute-start(f32[32,18,1,256]{3,0,2,1:T(8,128)S(1)} %get-tuple-element.13), channel_id=1, source_target_pairs={{0,1},{1,2},{2,3},{3,4},{4,5},{5,6},{6,7},{8,9},{9,10},{10,11},{11... | collective-permute-start | bytes 1769480 | tf_op jit(solution)/shard_map/ppermute | solution.py:27
  53.5 20.9 %copy-start.1 = (f32[32,16,8,256]{3,0,2,1:T(8,128)}, f32[32,16,8,256]{3,0,2,1:T(8,128)S(1)}, u32[]{:S(2)}) copy-start(f32[32,16,8,256]{3,0,2,1:T(8,128)S(1)} %fusion.2) | copy-start | bytes 12582916
  53.6 3.5 %collective-permute-start.5 = (f32[32,1,8,256]{3,0,2,1:T(8,128)S(1)}, f32[32,1,8,256]{3,0,2,1:T(8,128)S(1)}, u32[]{:S(2)}, u32[]{:S(2)}) collective-permute-start(f32[32,1,8,256]{3,0,2,1:T(8,128)S(1)} %get-tuple-element.14), channel_id=1, source_target_pairs={{0,8},{8,16},{16,24},{1,9},{9,17},{17,25},{2,10},{10,18},{18,26},{... | collective-permute-start | bytes 786440 | tf_op jit(solution)/shard_map/ppermute | solution.py:27
  55.8 4.1 %collective-permute-start.4 = (f32[32,1,8,256]{3,0,2,1:T(8,128)S(1)}, f32[32,1,8,256]{3,0,2,1:T(8,128)S(1)}, u32[]{:S(2)}, u32[]{:S(2)}) collective-permute-start(f32[32,1,8,256]{3,0,2,1:T(8,128)S(1)} %get-tuple-element.15), channel_id=1, source_target_pairs={{8,0},{16,8},{24,16},{9,1},{17,9},{25,17},{10,2},{18,10},{26,18},{... | collective-permute-start | bytes 786440 | tf_op jit(solution)/shard_map/ppermute | solution.py:29
  60.0 14.4 %collective-permute-start.6 = (f32[32,18,1,256]{3,0,2,1:T(8,128)S(1)}, f32[32,18,1,256]{3,0,2,1:T(8,128)S(1)}, u32[]{:S(2)}, u32[]{:S(2)}) collective-permute-start(f32[32,18,1,256]{3,0,2,1:T(8,128)S(1)} %get-tuple-element.10), channel_id=1, source_target_pairs={{1,0},{2,1},{3,2},{4,3},{5,4},{6,5},{7,6},{9,8},{10,9},{11,10},{12... | collective-permute-start | bytes 1769480 | tf_op jit(solution)/shard_map/ppermute | solution.py:29
  61.3 30.2 %collective-permute-start.7 = (f32[32,18,1,256]{3,0,2,1:T(8,128)S(1)}, f32[32,18,1,256]{3,0,2,1:T(8,128)S(1)}, u32[]{:S(2)}, u32[]{:S(2)}) collective-permute-start(f32[32,18,1,256]{3,0,2,1:T(8,128)S(1)} %get-tuple-element.11), channel_id=1, source_target_pairs={{0,1},{1,2},{2,3},{3,4},{4,5},{5,6},{6,7},{8,9},{9,10},{10,11},{11... | collective-permute-start | bytes 1769480 | tf_op jit(solution)/shard_map/ppermute | solution.py:27
  108.9 2.0 %copy-start = (f32[32,16,8,256]{3,0,2,1:T(8,128)}, f32[32,16,8,256]{3,0,2,1:T(8,128)S(1)}, u32[]{:S(2)}) copy-start(f32[32,16,8,256]{3,0,2,1:T(8,128)S(1)} %fusion.6) | copy-start | bytes 12582916
